TPU v7x, 256 devices: a whole 4x4x8 slice. The times are simulated.
256 devices in a mesh: sec: 4 (over z_hi, core), gx: 16 (over z_lo, y), gy: 4 (over x).
Axes of the slice: x: 4, y: 4, z: 8 (z_hi: 2, z_lo: 4; z = z_hi * 4 + z_lo), core: 2. Of those that a mesh axis runs over, the one named last changes fastest.
Arguments:
- fields: float32 [4, 3, 256, 8192], P('sec', None, 'gx', 'gy'), may hold values from -6 to 6
- x_ops: float32 [4, 3, 256, 256], P(None, None, 'gx'), may hold values from -4 to 4, as said below
- y_ops: float32 [4, 3, 256, 256], P(None, None, 'gy'), may hold values from -4 to 4, as said below
- x_line_class: int32 [256], P('gy'), may hold values from 0 to 3
- y_line_class: int32 [256], P('gx'), may hold values from 0 to 3
- box_offset: int32 [3, 2], replicated, may hold values from 0 to 63, as said below
- coupling: float32 [3, 3, 3], replicated, may hold values from -3 to 3
Outputs:
- fields_next: float32 [4, 3, 256, 8192], P('sec', None, 'gx', 'gy')
Inputs may be any that keep to these rules, and one draw needn't show every extreme that they name: `box_offset`: column 0 is below 16 and column 1 below 64; each column reaches its largest value for some box. `x_ops`: A dense matrix for each class and characteristic. `y_ops`: A dense matrix for each class and characteristic.
All inputs are finite; a program needn't handle non-finite values.
Results may differ from a plain program's by a relative error of at most 0.00013.
Values sent between devices are 32-bit elements; how exact they have to be, the bound alone decides.
A program may use at most 64 MiB of HBM per device.

v0:
```python
import jax
import jax.numpy as jnp
from jax import lax
from jax.sharding import PartitionSpec as P

CZ = 32
NCLASS = 4
STEPS = 2
time_step = 0.2
viscosity = 0.25
highest = lax.Precision.HIGHEST


def padded_2(block, sides, width):
    for axis, dim in sides:
        count = lax.axis_size(axis)
        forward = [(i, i + 1) for i in range(count - 1)]
        backward = [(target, source) for source, target in forward]
        low = lax.ppermute(
            lax.slice_in_dim(block, block.shape[dim] - width, None, axis=dim), axis, forward
        )
        high = lax.ppermute(lax.slice_in_dim(block, 0, width, axis=dim), axis, backward)
        block = jnp.concatenate([low, block, high], axis=dim)
    return block


def shifted(value, axis, steps):
    count = lax.axis_size(axis)
    initial, last = (max(0, -steps), min(count, count - steps))
    return lax.ppermute(value, axis, [(source, source + steps) for source in range(initial, last)])


def flow_core(padded):
    centre = padded[:, 1:-1, 1:-1, :]
    ahead_x = padded[:, 2:, 1:-1, :]
    behind_x = padded[:, :-2, 1:-1, :]
    ahead_y = padded[:, 1:-1, 2:, :]
    behind_y = padded[:, 1:-1, :-2, :]
    ahead_z = jnp.roll(centre, -1, axis=3)
    behind_z = jnp.roll(centre, 1, axis=3)
    slope_x = 0.5 * (ahead_x - behind_x)
    slope_y = 0.5 * (ahead_y - behind_y)
    slope_z = 0.5 * (ahead_z - behind_z)
    laplace = ahead_x + behind_x + ahead_y + behind_y + ahead_z + behind_z - 6.0 * centre
    omega_x = slope_y[2] - slope_z[1]
    omega_y = slope_z[0] - slope_x[2]
    omega_z = slope_x[1] - slope_y[0]
    lamb_vector = jnp.stack(
        [
            omega_y * centre[2] - omega_z * centre[1],
            omega_z * centre[0] - omega_x * centre[2],
            omega_x * centre[1] - omega_y * centre[0],
        ]
    )
    updated = centre + time_step * (viscosity * laplace - lamb_vector)
    return (updated, lamb_vector)


def skip_flow(padded):
    centre = padded[:, 1:-1, 1:-1, :]
    return (centre, jnp.zeros_like(centre))


def unchanged(accrued):
    return accrued


def place_source(padded_lamb, offset_x, offset_y, matrix, span_x, span_y, extent_x, extent_y):
    anchor = jnp.zeros((), jnp.int32)
    corner_x = span_x - offset_x - 1
    corner_y = span_y - offset_y - 1
    window = lax.dynamic_slice(
        padded_lamb,
        (anchor, corner_x, corner_y, anchor),
        (3, extent_x + 1, extent_y + 1, padded_lamb.shape[3]),
    )
    averaged = 0.25 * (
        window[:, :-1, :-1] + window[:, 1:, :-1] + window[:, :-1, 1:] + window[:, 1:, 1:]
    )
    return jnp.einsum("kj,jxyz->kxyz", matrix, averaged, precision=highest)


def sweep_lines_x(state, x_ops, select_x, active):
    initial = jnp.zeros(state.shape[1:], jnp.float32)

    def add_piece(running, portion, anchor):

        def work(accrued):
            partial_value = jnp.einsum("ckij,kjl->ckil", x_ops, portion[0], precision=highest)
            return jnp.sum(partial_value * select_x[:, None, None, :], axis=0)

        return lax.cond(active, work, unchanged, running)

    return add_piece(initial, lax.all_gather(state, "gx", axis=2, tiled=True), jnp.int32(0))


def sweep_lines_y(state, y_ops, select_y, active):
    initial = jnp.zeros(state.shape[1:], jnp.float32)

    def add_piece(running, portion, anchor):

        def work(accrued):
            partial_value = jnp.einsum("ckij,kxjz->ckxiz", y_ops, portion[0], precision=highest)
            return jnp.sum(partial_value * select_y[:, None, :, None, None], axis=0)

        return lax.cond(active, work, unchanged, running)

    return add_piece(initial, lax.all_gather(state, "gy", axis=3, tiled=True), jnp.int32(0))


def local(fields, x_ops, y_ops, x_line_class, y_line_class, box_offset, coupling):
    sections = lax.axis_size("sec")
    section_index = lax.axis_index("sec")
    active = section_index == sections - 1
    member = jnp.minimum(section_index, sections - 2)
    span_x = fields.shape[2]
    merged = fields.shape[3]
    span_y = merged // CZ
    classes = jnp.arange(NCLASS, dtype=jnp.int32)
    select_y = (classes[:, None] == y_line_class[None, :]).astype(jnp.float32)
    offsets = lax.dynamic_index_in_dim(box_offset, member, 0, keepdims=False)
    matrix = lax.dynamic_index_in_dim(coupling, member, 0, keepdims=False)
    current = fields[0].reshape(3, span_x, span_y, CZ)
    for repeat in range(STEPS):
        padded = padded_2(current, (("gx", 1), ("gy", 2)), 1)
        flowed, lamb_vector = lax.cond(active, skip_flow, flow_core, padded)
        left_tile = shifted(lamb_vector, "gx", 1)
        joined = jnp.concatenate([left_tile, lamb_vector], axis=1)
        lower_tile = shifted(joined, "gy", 1)
        joined = jnp.concatenate([lower_tile, joined], axis=2)
        contribution = place_source(
            joined, offsets[0], offsets[1], matrix, span_x, span_y, span_x, span_y
        )
        source = lax.psum(contribution, "sec")
        amplitudes_grid = current + time_step * source
        planes = amplitudes_grid.shape[3]
        merged_now = span_y * planes
        select_x = jnp.broadcast_to(
            (classes[:, None, None] == x_line_class[None, :, None]).astype(jnp.float32),
            (NCLASS, span_y, planes),
        ).reshape(NCLASS, merged_now)
        amplitudes = amplitudes_grid.reshape(1, 3, span_x, merged_now)
        swept_x = sweep_lines_x(amplitudes, x_ops, select_x, active)
        swept = sweep_lines_y(
            swept_x.reshape(1, 3, span_x, span_y, planes), y_ops, select_y, active
        )
        current = jnp.where(active, swept, flowed)
    return current.reshape(1, 3, span_x, merged)


def solution(mesh):
    placed = (
        P("sec", None, "gx", "gy"),
        P(None, None, "gx", None),
        P(None, None, "gy", None),
        P("gy"),
        P("gx"),
        P(),
        P(),
    )
    return jax.shard_map(
        local, mesh=mesh, in_specs=placed, out_specs=P("sec", None, "gx", "gy"), check_vma=False
    )
```

profile of v0, /device:TPU:129, one launch (start us, length us, event | category | flops | bytes accessed | tf_op | source)
XLA Modules:
  0.0 696.2 jit_solution(3194117666119599615)
XLA Ops:
  8.1 3.2 collective-permute-start
  13.1 3.6 collective-permute-done.1
  18.0 4.0 collective-permute-start.2
  26.2 3.1 pad_maximum_fusion.6
  29.3 2.4 conditional.6
  31.7 3.4 collective-permute-start.4
  35.1 9.2 %collective-permute-done.4 = f32[3,16,64,32]{2,3,1,0:T(8,128)S(1)} collective-permute-done((f32[3,16,64,32]{2,3,1,0:T(8,128)}, f32[3,16,64,32]{2,3,1,0:T(8,128)S(1)}, u32[]{:S(2)}, u32[]{:S(2)}) %collective-permute-start.4) | collective-permute-done | bytes 393248 | tf_op jit(solution)/shard_map/ppermute | solution.py:30
  44.4 4.3 collective-permute-start.5
  51.9 13.0 %collective-permute-done.5 = f32[3,32,64,32]{2,3,1,0:T(8,128)} collective-permute-done((f32[3,32,64,32]{2,3,1,0:T(8,128)S(1)}, f32[3,32,64,32]{2,3,1,0:T(8,128)}, u32[]{:S(2)}, u32[]{:S(2)}) %collective-permute-start.5) | collective-permute-done | bytes 786464 | tf_op jit(solution)/shard_map/ppermute | solution.py:30
  67.0 2.2 fusion.38
  70.9 97.7 %all-reduce.3.cloned.1.call-done = f32[3,16,64,32]{2,3,1,0:T(8,128)} async-done(((f32[3,16,64,32]{2,3,1,0:T(8,128)}), f32[3,16,64,32]{2,3,1,0:T(8,128)}) %all-reduce.3.cloned.1.call-update) | async-done | bytes 393232 | tf_op jit(solution)/shard_map/psum | solution.py:134
  172.0 83.1 %all-gather.5.cloned.1.call-done = f32[1,3,256,2048]{3,2,1,0:T(8,128)} async-done(((f32[1,3,16,2048]{3,2,1,0:T(8,128)}), f32[1,3,256,2048]{3,2,1,0:T(8,128)}) %all-gather.5.cloned.1.call-update) | async-done | bytes 6291472 | tf_op jit(solution)/shard_map/all_gather | solution.py:94
  255.2 7.1 %conditional.7 = (f32[3,16,2048]{2,1,0:T(8,128)S(1)}) conditional(s32[]{:T(128)} %convert_element_type.20, () %tuple.48, (f32[1,3,256,2048]{3,2,1,0:T(8,128)}, f32[4,3,16,256]{3,2,1,0:T(8,128)S(1)}, f32[4,64,32]{2,1,0:T(8,128)S(1)}) %tuple.131), branch_computations={%region_3.4_spmd, %region_4.6_spmd} | conditional | flops 1208647680 | bytes 6979592 | solution.py:92
  255.4 6.9 fusion.8
  264.2 68.8 %all-gather.7.cloned.1.call-done = f32[1,3,16,256,32]{4,3,2,1,0:T(8,128)} async-done(((f32[1,3,16,64,32]{4,3,2,1,0:T(8,128)}), f32[1,3,16,256,32]{4,3,2,1,0:T(8,128)}) %all-gather.7.cloned.1.call-update) | async-done | bytes 1572880 | tf_op jit(solution)/shard_map/all_gather | solution.py:108
  333.0 21.9 %conditional.8 = (f32[3,16,64,32]{2,3,1,0:T(8,128)S(1)}) conditional(s32[]{:T(128)} %convert_element_type.20, () %tuple.47, (f32[1,3,16,256,32]{4,3,2,1,0:T(8,128)}, f32[4,3,64,256]{3,2,1,0:T(8,128)S(1)}, f32[4,16]{0,1:T(8,128)S(1)}) %tuple.129), branch_computations={%region_6.7_spmd, %region_7.9_spmd} | conditional | flops 1208647680 | bytes 2752776 | solution.py:106
  333.0 21.9 %fusion.14 = f32[3,16,64,32]{2,3,1,0:T(8,128)S(1)} fusion(f32[1,3,16,256,32]{4,3,2,1,0:T(8,128)} %get-tuple-element.138, f32[4,16]{0,1:T(8,128)S(1)} %get-tuple-element.63, f32[4,3,64,256]{3,2,1,0:T(8,128)S(1)} %get-tuple-element.139), kind=kOutput, calls=%fused_computation.22 | convolution fusion | flops 1208647680 | bytes 2752768 | tf_op jit(solution)/shard_map/cond/branch_1_fun/ckij,kxjz->ckxiz/dot_general | solution.py:103
  355.1 3.1 collective-permute-start.6
  359.6 3.5 collective-permute-done.7
  364.8 2.8 collective-permute-start.8
  369.7 2.9 collective-permute-done.9
  375.0 3.2 collective-permute-start.10
  378.1 17.3 %collective-permute-done.10 = f32[3,16,64,32]{2,3,1,0:T(8,128)S(1)} collective-permute-done((f32[3,16,64,32]{2,3,1,0:T(8,128)S(1)}, f32[3,16,64,32]{2,3,1,0:T(8,128)S(1)}, u32[]{:S(2)}, u32[]{:S(2)}) %collective-permute-start.10) | collective-permute-done | bytes 393248 | tf_op jit(solution)/shard_map/ppermute | solution.py:30
  395.6 2.9 collective-permute-start.11
  398.5 33.3 %collective-permute-done.11 = f32[3,32,64,32]{2,3,1,0:T(8,128)S(1)} collective-permute-done((f32[3,32,64,32]{2,3,1,0:T(8,128)S(1)}, f32[3,32,64,32]{2,3,1,0:T(8,128)S(1)}, u32[]{:S(2)}, u32[]{:S(2)}) %collective-permute-start.11) | collective-permute-done | bytes 786464 | tf_op jit(solution)/shard_map/ppermute | solution.py:30
  436.0 64.7 %all-reduce.5.cloned.1.call-done = f32[3,16,64,32]{2,3,1,0:T(8,128)} async-done(((f32[3,16,64,32]{2,3,1,0:T(8,128)}), f32[3,16,64,32]{2,3,1,0:T(8,128)}) %all-reduce.5.cloned.1.call-update) | async-done | bytes 393232 | tf_op jit(solution)/shard_map/psum | solution.py:134
  504.1 83.2 %all-gather.9.cloned.1.call-done = f32[1,3,256,2048]{3,2,1,0:T(8,128)} async-done(((f32[1,3,16,2048]{3,2,1,0:T(8,128)}), f32[1,3,256,2048]{3,2,1,0:T(8,128)}) %all-gather.9.cloned.1.call-update) | async-done | bytes 6291472 | tf_op jit(solution)/shard_map/all_gather | solution.py:94
  587.2 7.2 %conditional.10 = (f32[3,16,2048]{2,1,0:T(8,128)S(1)}) conditional(s32[]{:T(128)} %convert_element_type.20, () %tuple.46, (f32[1,3,256,2048]{3,2,1,0:T(8,128)}, f32[4,3,16,256]{3,2,1,0:T(8,128)S(1)}, f32[4,64,32]{2,1,0:T(8,128)S(1)}) %tuple.132), branch_computations={%region_12.13_spmd, %region_13.15_spmd} | conditional | flops 1208647680 | bytes 6979592 | solution.py:92
  587.5 6.9 fusion.26
  596.2 68.9 %all-gather.11.cloned.1.call-done = f32[1,3,16,256,32]{4,3,2,1,0:T(8,128)} async-done(((f32[1,3,16,64,32]{4,3,2,1,0:T(8,128)}), f32[1,3,16,256,32]{4,3,2,1,0:T(8,128)}) %all-gather.11.cloned.1.call-update) | async-done | bytes 1572880 | tf_op jit(solution)/shard_map/all_gather | solution.py:108
  665.1 21.9 %conditional.11 = (f32[3,16,64,32]{2,3,1,0:T(8,128)S(1)}) conditional(s32[]{:T(128)} %convert_element_type.20, () %tuple.45, (f32[1,3,16,256,32]{4,3,2,1,0:T(8,128)}, f32[4,3,64,256]{3,2,1,0:T(8,128)S(1)}, f32[4,16]{0,1:T(8,128)S(1)}) %tuple.130), branch_computations={%region_15.16_spmd, %region_16.18_spmd} | conditional | flops 1208647680 | bytes 2752776 | solution.py:106
  665.1 21.9 %fusion.32 = f32[3,16,64,32]{2,3,1,0:T(8,128)S(1)} fusion(f32[1,3,16,256,32]{4,3,2,1,0:T(8,128)} %get-tuple-element.147, f32[4,16]{0,1:T(8,128)S(1)} %get-tuple-element.72, f32[4,3,64,256]{3,2,1,0:T(8,128)S(1)} %get-tuple-element.148), kind=kOutput, calls=%fused_computation.46 | convolution fusion | flops 1208647680 | bytes 2752768 | tf_op jit(solution)/shard_map/cond/branch_1_fun/ckij,kxjz->ckxiz/dot_general | solution.py:103
  (100 shorter events, 40.6 us)
Async XLA Ops:
  6.5 60.5 %copy-start = (f32[3,3,3]{2,1,0:T(4,128)S(1)}, f32[3,3,3]{2,1,0:T(4,128)}, u32[]{:S(2)}) copy-start(f32[3,3,3]{2,1,0:T(4,128)} %param.25) | copy-start | bytes 328
  6.5 162.0 %all-reduce.3.cloned.1.call-start = ((), (), s32[]{:S(2)}) async-start(), calls=%async_computation | async-start | bytes 1572864 | tf_op jit(solution)/shard_map/psum | solution.py:134
  8.1 4.8 collective-permute-start
  11.3 5.4 collective-permute-start.1
  16.7 6.7 collective-permute-start.3
  18.0 6.8 collective-permute-start.2
  31.7 12.6 %copy-start.11 = (f32[3,16,64,32]{2,3,1,0:T(8,128)S(1)}, f32[3,16,64,32]{2,3,1,0:T(8,128)}, u32[]{:S(2)}) copy-start(f32[3,16,64,32]{2,3,1,0:T(8,128)} %get-tuple-element.150) | copy-start | bytes 1179652
  31.7 17.0 %copy-start.14 = (s32[3,2]{0,1:T(2,128)S(1)}, s32[3,2]{0,1:T(2,128)}, u32[]{:S(2)}) copy-start(s32[3,2]{0,1:T(2,128)} %param.24) | copy-start | bytes 76
  31.7 12.6 %collective-permute-start.4 = (f32[3,16,64,32]{2,3,1,0:T(8,128)}, f32[3,16,64,32]{2,3,1,0:T(8,128)S(1)}, u32[]{:S(2)}, u32[]{:S(2)}) collective-permute-start(f32[3,16,64,32]{2,3,1,0:T(8,128)} %get-tuple-element.150), channel_id=1, source_target_pairs={{0,4},{4,8},{8,12},{12,16},{16,20},{20,24},{24,28},{28,32},{32,36}... | collective-permute-start | bytes 1179656 | tf_op jit(solution)/shard_map/ppermute | solution.py:30
  44.4 20.5 %collective-permute-start.5 = (f32[3,32,64,32]{2,3,1,0:T(8,128)S(1)}, f32[3,32,64,32]{2,3,1,0:T(8,128)}, u32[]{:S(2)}, u32[]{:S(2)}) collective-permute-start(f32[3,32,64,32]{2,3,1,0:T(8,128)S(1)} %constant_dynamic-update-slice_fusion.3), channel_id=1, source_target_pairs={{0,1},{1,2},{2,3},{4,5},{5,6},{6,7},{8,9},{9,10},{10,11},{12,13},{... | collective-permute-start | bytes 2359304 | tf_op jit(solution)/shard_map/ppermute | solution.py:30
  70.2 184.9 %all-gather.5.cloned.1.call-start = ((), (), s32[]{:S(2)}) async-start(), calls=%async_computation.1 | async-start | bytes 6684672 | tf_op jit(solution)/shard_map/all_gather | solution.py:94
  170.4 1.6 copy-start.15
  170.4 84.8 %copy-start.12 = (f32[4,3,16,256]{3,2,1,0:T(8,128)S(1)}, f32[4,3,16,256]{3,2,1,0:T(8,128)}, u32[]{:S(2)}) copy-start(f32[4,3,16,256]{3,2,1,0:T(8,128)} %param.20) | copy-start | bytes 589828
  171.9 161.1 %all-gather.7.cloned.1.call-start = ((), (), s32[]{:S(2)}) async-start(), calls=%async_computation.2 | async-start | bytes 7864320 | tf_op jit(solution)/shard_map/all_gather | solution.py:108
  262.3 1.8 copy-start.16
  262.3 70.7 %copy-start.8 = (f32[4,3,64,256]{3,2,1,0:T(8,128)S(1)}, f32[4,3,64,256]{3,2,1,0:T(8,128)}, u32[]{:S(2)}) copy-start(f32[4,3,64,256]{3,2,1,0:T(8,128)} %param.21) | copy-start | bytes 2359300
  264.1 236.6 %all-reduce.5.cloned.1.call-start = ((), (), s32[]{:S(2)}) async-start(), calls=%async_computation.3 | async-start | bytes 1572864 | tf_op jit(solution)/shard_map/psum | solution.py:134
  333.0 22.0 %copy-start.10 = (f32[3,16,64,32]{2,3,1,0:T(8,128)S(1)}, f32[3,16,64,32]{2,3,1,0:T(8,128)}, u32[]{:S(2)}) copy-start(f32[3,16,64,32]{2,3,1,0:T(8,128)} %get-tuple-element.151) | copy-start | bytes 1179652
  355.1 19.3 %copy-start.3 = (f32[3,16,64,32]{2,3,1,0:T(8,128)}, f32[3,16,64,32]{2,3,1,0:T(8,128)S(1)}, u32[]{:S(2)}) copy-start(f32[3,16,64,32]{2,3,1,0:T(8,128)S(1)} %broadcast_select_fusion.1) | copy-start | bytes 1179652
  355.1 4.4 collective-permute-start.6
  358.2 4.8 collective-permute-start.7
  363.2 0.9 copy-start.5
  364.8 4.5 collective-permute-start.8
  368.0 4.6 collective-permute-start.9
  375.0 20.5 %collective-permute-start.10 = (f32[3,16,64,32]{2,3,1,0:T(8,128)S(1)}, f32[3,16,64,32]{2,3,1,0:T(8,128)S(1)}, u32[]{:S(2)}, u32[]{:S(2)}) collective-permute-start(f32[3,16,64,32]{2,3,1,0:T(8,128)S(1)} %get-tuple-element.152), channel_id=1, source_target_pairs={{0,4},{4,8},{8,12},{12,16},{16,20},{20,24},{24,28},{28,32},{32,36}... | collective-permute-start | bytes 1179656 | tf_op jit(solution)/shard_map/ppermute | solution.py:30
  395.6 36.2 %collective-permute-start.11 = (f32[3,32,64,32]{2,3,1,0:T(8,128)S(1)}, f32[3,32,64,32]{2,3,1,0:T(8,128)S(1)}, u32[]{:S(2)}, u32[]{:S(2)}) collective-permute-start(f32[3,32,64,32]{2,3,1,0:T(8,128)S(1)} %constant_dynamic-update-slice_fusion.5), channel_id=1, source_target_pairs={{0,1},{1,2},{2,3},{4,5},{5,6},{6,7},{8,9},{9,10},{10,11},{12,13},{... | collective-permute-start | bytes 2359304 | tf_op jit(solution)/shard_map/ppermute | solution.py:30
  435.0 65.7 %copy-start.4 = (f32[3,16,64,32]{2,3,1,0:T(8,128)S(1)}, f32[3,16,64,32]{2,3,1,0:T(8,128)}, u32[]{:S(2)}) copy-start(f32[3,16,64,32]{2,3,1,0:T(8,128)} %copy-done.3) | copy-start | bytes 1179652
  436.0 151.2 %all-gather.9.cloned.1.call-start = ((), (), s32[]{:S(2)}) async-start(), calls=%async_computation.4 | async-start | bytes 6684672 | tf_op jit(solution)/shard_map/all_gather | solution.py:94
  502.5 84.7 %copy-start.13 = (f32[4,3,16,256]{3,2,1,0:T(8,128)S(1)}, f32[4,3,16,256]{3,2,1,0:T(8,128)}, u32[]{:S(2)}) copy-start(f32[4,3,16,256]{3,2,1,0:T(8,128)} %param.20) | copy-start | bytes 589828
  504.0 161.1 %all-gather.11.cloned.1.call-start = ((), (), s32[]{:S(2)}) async-start(), calls=%async_computation.5 | async-start | bytes 7864320 | tf_op jit(solution)/shard_map/all_gather | solution.py:108
  594.4 70.7 %copy-start.9 = (f32[4,3,64,256]{3,2,1,0:T(8,128)S(1)}, f32[4,3,64,256]{3,2,1,0:T(8,128)}, u32[]{:S(2)}) copy-start(f32[4,3,64,256]{3,2,1,0:T(8,128)} %param.21) | copy-start | bytes 2359300
Sparse Core Ops, SparseCore 0:
  70.4 98.1 all-reduce.2
  172.0 83.0 all-gather.4
  264.2 68.7 all-gather.6
  436.1 64.5 all-reduce.4
  504.1 83.0 all-gather.8
  596.3 68.7 all-gather.10
where the time goes:
time: 705 us; the launch traced here: 696 us
  waiting for transfers between devices  549 us (78%)
  matrix products  62.1 us (9%)
  starting transfers between devices  32.4 us (5%)
  local copies, waits for them, and re-layouts  24.3 us (3%)
  between operations  16.6 us (2%)
  other arithmetic  10.8 us (2%)
    all_gather x2, waiting for transfers between devices, sweep_lines_x(): lax.all_gather(state, 'gx', axis=2, tiled=True)  166 us
    psum x2, waiting for transfers between devices, local(): source = lax.psum(contribution, 'sec')  162 us
    all_gather x2, waiting for transfers between devices, sweep_lines_y(): lax.all_gather(state, 'gy', axis=3, tiled=True)  138 us
    ppermute x4, waiting for transfers between devices, shifted(): lax.ppermute(value, axis, [(source, source + steps) for source in range(i...  72.8 us
    dot_general x2, matrix products, work(): jnp.einsum('ckij,kxjz->ckxiz', y_ops, portion[0], precision=highest)  43.8 us
  transfers between devices with their start and end apart: 18, of which 14 were waited for; matrix products, arithmetic and copies ran while one was open for 1% of the time, Pallas kernels for 0%

commit v1 on v0

--- a/solution.py
+++ b/solution.py
@@ -9,6 +9,11 @@
 time_step = 0.2
 viscosity = 0.25
 highest = lax.Precision.HIGHEST
+
+
+def all_by_exchange(array, name, d):
+    sent = jnp.stack([array] * lax.axis_size(name))
+    return jnp.concatenate(lax.all_to_all(sent, name, 0, 0), axis=d)
 
 
 def padded_2(block, sides, width):
@@ -91,7 +96,7 @@
 
         return lax.cond(active, work, unchanged, running)
 
-    return add_piece(initial, lax.all_gather(state, "gx", axis=2, tiled=True), jnp.int32(0))
+    return add_piece(initial, all_by_exchange(state, "gx", 2), jnp.int32(0))
 
 
 def sweep_lines_y(state, y_ops, select_y, active):

time: 705 us -> 829 us (1.18)
  waiting for transfers between devices: 549 us -> 659 us
  local copies, waits for them, and re-layouts: 24.3 us -> 35.7 us
  starting transfers between devices: 32.4 us -> 43 us
    all_to_all x0 -> x2, waiting for transfers between devices: none -> 231 us  [all_by_exchange(): return jnp.concatenate(lax.all_to_all(sent, name, 0, 0), axis=d)]
    all_gather x2 -> x0, waiting for transfers between devices: 166 us -> none  [sweep_lines_x(): lax.all_gather(state, 'gx', axis=2, tiled=True)]
    all_gather x2, waiting for transfers between devices: 138 us -> 183 us  [sweep_lines_y(): lax.all_gather(state, 'gy', axis=3, tiled=True)]
    another operation x2 -> x8, local copies, waits for them, and re-layouts: 1.09 us -> 15.9 us  [the longest x4 8.42 us: all_by_exchange(): sent = jnp.stack([array] * lax.axis_size(name))]
    all_to_all x0 -> x2, starting transfers between devices: none -> 10.7 us  [all_by_exchange(): return jnp.concatenate(lax.all_to_all(sent, name, 0, 0), axis=d)]
where the time goes in v1:
time: 829 us; the launch traced here: 822 us
  waiting for transfers between devices  659 us (79%)
  matrix products  56.6 us (7%)
  starting transfers between devices  43 us (5%)
  local copies, waits for them, and re-layouts  35.7 us (4%)
  between operations  16.3 us (2%)
  other arithmetic  10.8 us (1%)
    all_to_all x2, waiting for transfers between devices, all_by_exchange(): return jnp.concatenate(lax.all_to_all(sent, name, 0, 0), axis=d)  231 us
    all_gather x2, waiting for transfers between devices, sweep_lines_y(): lax.all_gather(state, 'gy', axis=3, tiled=True)  183 us
    psum x2, waiting for transfers between devices, local(): source = lax.psum(contribution, 'sec')  162 us
    ppermute x4, waiting for transfers between devices, shifted(): lax.ppermute(value, axis, [(source, source + steps) for source in range(i...  72.5 us
    dot_general x2, matrix products, work(): jnp.einsum('ckij,kxjz->ckxiz', y_ops, portion[0], precision=highest)  43.8 us
  transfers between devices with their start and end apart: 18, of which 14 were waited for; matrix products, arithmetic and copies ran while one was open for 1% of the time, Pallas kernels for 0%

profile of v1, /device:TPU:129, one launch (start us, length us, event | category | flops | bytes accessed | tf_op | source)
XLA Modules:
  0.0 822.2 jit_solution(6178038010264980018)
XLA Ops:
  8.1 3.2 collective-permute-start
  13.1 3.6 collective-permute-done.1
  18.0 4.0 collective-permute-start.2
  26.1 3.1 pad_maximum_fusion.6
  31.6 3.4 collective-permute-start.4
  35.0 9.2 %collective-permute-done.4 = f32[3,16,64,32]{2,3,1,0:T(8,128)S(1)} collective-permute-done((f32[3,16,64,32]{2,3,1,0:T(8,128)}, f32[3,16,64,32]{2,3,1,0:T(8,128)S(1)}, u32[]{:S(2)}, u32[]{:S(2)}) %collective-permute-start.4) | collective-permute-done | bytes 393248 | tf_op jit(solution)/shard_map/ppermute | solution.py:35
  44.3 4.4 collective-permute-start.5
  51.9 12.8 %collective-permute-done.5 = f32[3,32,64,32]{2,3,1,0:T(8,128)} collective-permute-done((f32[3,32,64,32]{2,3,1,0:T(8,128)S(1)}, f32[3,32,64,32]{2,3,1,0:T(8,128)}, u32[]{:S(2)}, u32[]{:S(2)}) %collective-permute-start.5) | collective-permute-done | bytes 786464 | tf_op jit(solution)/shard_map/ppermute | solution.py:35
  70.6 97.9 %all-reduce.3.cloned.1.call-done = f32[3,16,64,32]{2,3,1,0:T(8,128)} async-done(((f32[3,16,64,32]{2,3,1,0:T(8,128)}), f32[3,16,64,32]{2,3,1,0:T(8,128)}) %all-reduce.3.cloned.1.call-update) | async-done | bytes 393232 | tf_op jit(solution)/shard_map/psum | solution.py:139
  171.0 3.5 stack.12
  174.5 5.3 all-to-all-start
  179.9 115.3 %all-to-all-done = f32[16,1,3,16,2048]{4,3,2,1,0:T(8,128)} async-done(((f32[16,1,3,16,2048]{4,3,2,1,0:T(8,128)}), f32[16,1,3,16,2048]{4,3,2,1,0:T(8,128)}, u32[]{:S(2)}, u32[]{:S(2)}) %all-to-all-start) | async-done | bytes 6291488 | tf_op jit(solution)/shard_map/all_to_all | solution.py:16
  295.3 7.6 conditional.7
  295.5 3.2 copy.90
  298.7 4.2 fusion.1
  304.8 91.5 %all-gather.3.cloned.1.call-done = f32[1,3,16,256,32]{4,3,2,1,0:T(8,128)} async-done(((f32[1,3,16,64,32]{4,3,2,1,0:T(8,128)}), f32[1,3,16,256,32]{4,3,2,1,0:T(8,128)}) %all-gather.3.cloned.1.call-update) | async-done | bytes 1572880 | tf_op jit(solution)/shard_map/all_gather | solution.py:113
  396.3 22.1 %conditional.8 = (f32[3,16,64,32]{2,3,1,0:T(8,128)S(1)}) conditional(s32[]{:T(128)} %convert_element_type.20, () %tuple.47, (f32[1,3,16,256,32]{4,3,2,1,0:T(8,128)}, f32[4,3,64,256]{3,2,1,0:T(8,128)S(1)}, f32[4,16]{0,1:T(8,128)S(1)}) %tuple.125), branch_computations={%region_6.7_spmd, %region_7.9_spmd} | conditional | flops 1208647680 | bytes 2752776 | solution.py:111
  396.5 21.9 %fusion.5 = f32[3,16,64,32]{2,3,1,0:T(8,128)S(1)} fusion(f32[1,3,16,256,32]{4,3,2,1,0:T(8,128)} %get-tuple-element.138, f32[4,16]{0,1:T(8,128)S(1)} %get-tuple-element.63, f32[4,3,64,256]{3,2,1,0:T(8,128)S(1)} %get-tuple-element.139), kind=kOutput, calls=%fused_computation.20 | convolution fusion | flops 1208647680 | bytes 2752768 | tf_op jit(solution)/shard_map/cond/branch_1_fun/ckij,kxjz->ckxiz/dot_general | solution.py:108
  423.0 3.5 collective-permute-done.7
  438.1 3.2 collective-permute-start.10
  441.3 17.1 %collective-permute-done.10 = f32[3,16,64,32]{2,3,1,0:T(8,128)S(1)} collective-permute-done((f32[3,16,64,32]{2,3,1,0:T(8,128)S(1)}, f32[3,16,64,32]{2,3,1,0:T(8,128)S(1)}, u32[]{:S(2)}, u32[]{:S(2)}) %collective-permute-start.10) | collective-permute-done | bytes 393248 | tf_op jit(solution)/shard_map/ppermute | solution.py:35
  461.4 33.5 %collective-permute-done.11 = f32[3,32,64,32]{2,3,1,0:T(8,128)S(1)} collective-permute-done((f32[3,32,64,32]{2,3,1,0:T(8,128)S(1)}, f32[3,32,64,32]{2,3,1,0:T(8,128)S(1)}, u32[]{:S(2)}, u32[]{:S(2)}) %collective-permute-start.11) | collective-permute-done | bytes 786464 | tf_op jit(solution)/shard_map/ppermute | solution.py:35
  499.1 64.5 %all-reduce.5.cloned.1.call-done = f32[3,16,64,32]{2,3,1,0:T(8,128)} async-done(((f32[3,16,64,32]{2,3,1,0:T(8,128)}), f32[3,16,64,32]{2,3,1,0:T(8,128)}) %all-reduce.5.cloned.1.call-update) | async-done | bytes 393232 | tf_op jit(solution)/shard_map/psum | solution.py:139
  566.1 3.5 stack.17
  569.6 5.3 all-to-all-start.1
  575.0 115.3 %all-to-all-done.1 = f32[16,1,3,16,2048]{4,3,2,1,0:T(8,128)} async-done(((f32[16,1,3,16,2048]{4,3,2,1,0:T(8,128)}), f32[16,1,3,16,2048]{4,3,2,1,0:T(8,128)}, u32[]{:S(2)}, u32[]{:S(2)}) %all-to-all-start.1) | async-done | bytes 6291488 | tf_op jit(solution)/shard_map/all_to_all | solution.py:16
  690.3 7.7 conditional.10
  690.6 3.2 copy.108
  693.8 4.2 fusion.10
  699.8 91.6 %all-gather.5.cloned.1.call-done = f32[1,3,16,256,32]{4,3,2,1,0:T(8,128)} async-done(((f32[1,3,16,64,32]{4,3,2,1,0:T(8,128)}), f32[1,3,16,256,32]{4,3,2,1,0:T(8,128)}) %all-gather.5.cloned.1.call-update) | async-done | bytes 1572880 | tf_op jit(solution)/shard_map/all_gather | solution.py:113
  791.4 21.9 %conditional.11 = (f32[3,16,64,32]{2,3,1,0:T(8,128)S(1)}) conditional(s32[]{:T(128)} %convert_element_type.20, () %tuple.45, (f32[1,3,16,256,32]{4,3,2,1,0:T(8,128)}, f32[4,3,64,256]{3,2,1,0:T(8,128)S(1)}, f32[4,16]{0,1:T(8,128)S(1)}) %tuple.126), branch_computations={%region_15.16_spmd, %region_16.18_spmd} | conditional | flops 1208647680 | bytes 2752776 | solution.py:111
  791.4 21.9 %fusion.14 = f32[3,16,64,32]{2,3,1,0:T(8,128)S(1)} fusion(f32[1,3,16,256,32]{4,3,2,1,0:T(8,128)} %get-tuple-element.147, f32[4,16]{0,1:T(8,128)S(1)} %get-tuple-element.72, f32[4,3,64,256]{3,2,1,0:T(8,128)S(1)} %get-tuple-element.148), kind=kOutput, calls=%fused_computation.42 | convolution fusion | flops 1208647680 | bytes 2752768 | tf_op jit(solution)/shard_map/cond/branch_1_fun/ckij,kxjz->ckxiz/dot_general | solution.py:108
  (102 shorter events, 54.6 us)
Async XLA Ops:
  6.5 60.4 %copy-start = (f32[3,3,3]{2,1,0:T(4,128)S(1)}, f32[3,3,3]{2,1,0:T(4,128)}, u32[]{:S(2)}) copy-start(f32[3,3,3]{2,1,0:T(4,128)} %param.25) | copy-start | bytes 328
  6.5 161.9 %all-reduce.3.cloned.1.call-start = ((), (), s32[]{:S(2)}) async-start(), calls=%async_computation.2 | async-start | bytes 1572864 | tf_op jit(solution)/shard_map/psum | solution.py:139
  8.1 4.8 collective-permute-start
  11.3 5.4 collective-permute-start.1
  16.7 6.7 collective-permute-start.3
  18.0 6.8 collective-permute-start.2
  31.6 12.6 %copy-start.11 = (f32[3,16,64,32]{2,3,1,0:T(8,128)S(1)}, f32[3,16,64,32]{2,3,1,0:T(8,128)}, u32[]{:S(2)}) copy-start(f32[3,16,64,32]{2,3,1,0:T(8,128)} %get-tuple-element.150) | copy-start | bytes 1179652
  31.6 17.1 %copy-start.14 = (s32[3,2]{0,1:T(2,128)S(1)}, s32[3,2]{0,1:T(2,128)}, u32[]{:S(2)}) copy-start(s32[3,2]{0,1:T(2,128)} %param.24) | copy-start | bytes 76
  31.6 12.6 %collective-permute-start.4 = (f32[3,16,64,32]{2,3,1,0:T(8,128)}, f32[3,16,64,32]{2,3,1,0:T(8,128)S(1)}, u32[]{:S(2)}, u32[]{:S(2)}) collective-permute-start(f32[3,16,64,32]{2,3,1,0:T(8,128)} %get-tuple-element.150), channel_id=1, source_target_pairs={{0,4},{4,8},{8,12},{12,16},{16,20},{20,24},{24,28},{28,32},{32,36}... | collective-permute-start | bytes 1179656 | tf_op jit(solution)/shard_map/ppermute | solution.py:35
  44.3 20.5 %collective-permute-start.5 = (f32[3,32,64,32]{2,3,1,0:T(8,128)S(1)}, f32[3,32,64,32]{2,3,1,0:T(8,128)}, u32[]{:S(2)}, u32[]{:S(2)}) collective-permute-start(f32[3,32,64,32]{2,3,1,0:T(8,128)S(1)} %constant_dynamic-update-slice_fusion.3), channel_id=1, source_target_pairs={{0,1},{1,2},{2,3},{4,5},{5,6},{6,7},{8,9},{9,10},{10,11},{12,13},{... | collective-permute-start | bytes 2359304 | tf_op jit(solution)/shard_map/ppermute | solution.py:35
  174.5 5.4 copy-start.15
  174.5 120.8 %copy-start.12 = (f32[4,3,16,256]{3,2,1,0:T(8,128)S(1)}, f32[4,3,16,256]{3,2,1,0:T(8,128)}, u32[]{:S(2)}) copy-start(f32[4,3,16,256]{3,2,1,0:T(8,128)} %param.20) | copy-start | bytes 589828
  174.5 120.7 %all-to-all-start = ((f32[16,1,3,16,2048]{4,3,2,1,0:T(8,128)}), f32[16,1,3,16,2048]{4,3,2,1,0:T(8,128)}, u32[]{:S(2)}, u32[]{:S(2)}) async-start(f32[16,1,3,16,2048]{4,3,2,1,0:T(8,128)} %stack.12), calls=%async_computation | async-start | bytes 12582912 | tf_op jit(solution)/shard_map/all_to_all | solution.py:16
  179.8 216.5 %all-gather.3.cloned.1.call-start = ((), (), s32[]{:S(2)}) async-start(), calls=%async_computation.3 | async-start | bytes 7864320 | tf_op jit(solution)/shard_map/all_gather | solution.py:113
  302.9 1.8 copy-start.16
  302.9 93.4 %copy-start.8 = (f32[4,3,64,256]{3,2,1,0:T(8,128)S(1)}, f32[4,3,64,256]{3,2,1,0:T(8,128)}, u32[]{:S(2)}) copy-start(f32[4,3,64,256]{3,2,1,0:T(8,128)} %param.21) | copy-start | bytes 2359300
  304.7 258.9 %all-reduce.5.cloned.1.call-start = ((), (), s32[]{:S(2)}) async-start(), calls=%async_computation.4 | async-start | bytes 1572864 | tf_op jit(solution)/shard_map/psum | solution.py:139
  396.3 22.1 %copy-start.10 = (f32[3,16,64,32]{2,3,1,0:T(8,128)S(1)}, f32[3,16,64,32]{2,3,1,0:T(8,128)}, u32[]{:S(2)}) copy-start(f32[3,16,64,32]{2,3,1,0:T(8,128)} %get-tuple-element.151) | copy-start | bytes 1179652
  418.6 19.0 %copy-start.3 = (f32[3,16,64,32]{2,3,1,0:T(8,128)}, f32[3,16,64,32]{2,3,1,0:T(8,128)S(1)}, u32[]{:S(2)}) copy-start(f32[3,16,64,32]{2,3,1,0:T(8,128)S(1)} %broadcast_select_fusion.1) | copy-start | bytes 1179652
  418.6 4.4 collective-permute-start.6
  421.7 4.8 collective-permute-start.7
  426.6 0.9 copy-start.5
  427.9 4.5 collective-permute-start.8
  431.1 4.6 collective-permute-start.9
  438.1 20.2 %collective-permute-start.10 = (f32[3,16,64,32]{2,3,1,0:T(8,128)S(1)}, f32[3,16,64,32]{2,3,1,0:T(8,128)S(1)}, u32[]{:S(2)}, u32[]{:S(2)}) collective-permute-start(f32[3,16,64,32]{2,3,1,0:T(8,128)S(1)} %get-tuple-element.152), channel_id=1, source_target_pairs={{0,4},{4,8},{8,12},{12,16},{16,20},{20,24},{24,28},{28,32},{32,36}... | collective-permute-start | bytes 1179656 | tf_op jit(solution)/shard_map/ppermute | solution.py:35
  458.5 36.4 %collective-permute-start.11 = (f32[3,32,64,32]{2,3,1,0:T(8,128)S(1)}, f32[3,32,64,32]{2,3,1,0:T(8,128)S(1)}, u32[]{:S(2)}, u32[]{:S(2)}) collective-permute-start(f32[3,32,64,32]{2,3,1,0:T(8,128)S(1)} %constant_dynamic-update-slice_fusion.5), channel_id=1, source_target_pairs={{0,1},{1,2},{2,3},{4,5},{5,6},{6,7},{8,9},{9,10},{10,11},{12,13},{... | collective-permute-start | bytes 2359304 | tf_op jit(solution)/shard_map/ppermute | solution.py:35
  498.0 65.5 %copy-start.4 = (f32[3,16,64,32]{2,3,1,0:T(8,128)S(1)}, f32[3,16,64,32]{2,3,1,0:T(8,128)}, u32[]{:S(2)}) copy-start(f32[3,16,64,32]{2,3,1,0:T(8,128)} %copy-done.3) | copy-start | bytes 1179652
  569.6 120.7 %copy-start.13 = (f32[4,3,16,256]{3,2,1,0:T(8,128)S(1)}, f32[4,3,16,256]{3,2,1,0:T(8,128)}, u32[]{:S(2)}) copy-start(f32[4,3,16,256]{3,2,1,0:T(8,128)} %param.20) | copy-start | bytes 589828
  569.6 120.7 %all-to-all-start.1 = ((f32[16,1,3,16,2048]{4,3,2,1,0:T(8,128)}), f32[16,1,3,16,2048]{4,3,2,1,0:T(8,128)}, u32[]{:S(2)}, u32[]{:S(2)}) async-start(f32[16,1,3,16,2048]{4,3,2,1,0:T(8,128)} %stack.17), calls=%async_computation.1 | async-start | bytes 12582912 | tf_op jit(solution)/shard_map/all_to_all | solution.py:16
  574.9 216.5 %all-gather.5.cloned.1.call-start = ((), (), s32[]{:S(2)}) async-start(), calls=%async_computation.5 | async-start | bytes 7864320 | tf_op jit(solution)/shard_map/all_gather | solution.py:113
  698.0 93.4 %copy-start.9 = (f32[4,3,64,256]{3,2,1,0:T(8,128)S(1)}, f32[4,3,64,256]{3,2,1,0:T(8,128)}, u32[]{:S(2)}) copy-start(f32[4,3,64,256]{3,2,1,0:T(8,128)} %param.21) | copy-start | bytes 2359300
Sparse Core Ops, SparseCore 0:
  70.2 98.1 all-reduce.2
  304.8 91.4 all-gather.2
  499.2 64.3 all-reduce.4
  699.9 91.4 all-gather.4
